TPU v7x, 32 devices: a whole 2x2x4 slice. The times are simulated.
32 devices in a mesh: segment: 8 (over z, y), band: 4 (over x, core).
Axes of the slice: x: 2, y: 2, z: 4, core: 2. Of those that a mesh axis runs over, the one named last changes fastest.
Arguments:
- forward_state: bfloat16 [8, 2, 32, 64, 256], P('segment', None, 'band'), may hold values from -6 to 6
- returning_state: bfloat16 [8, 2, 32, 64, 256], P('segment', None, 'band'), may hold values from -6 to 6
- returning_grad: bfloat16 [8, 2, 32, 64, 256], P('segment', None, 'band'), may hold values from -6 to 6
- weights: bfloat16 [8, 2, 2304, 256], P('segment'), may hold values from -0.125 to 0.125
- fresh_input: bfloat16 [2, 2, 32, 64, 256], P(None, None, 'band'), may hold values from -6 to 6
- loss_grad: bfloat16 [2, 2, 32, 64, 256], P(None, None, 'band'), may hold values from -6 to 6
Outputs:
- forward_out: bfloat16 [8, 2, 32, 64, 256], P('segment', None, 'band')
- returning_out: bfloat16 [8, 2, 32, 64, 256], P('segment', None, 'band')
- backward_out: bfloat16 [8, 2, 32, 64, 256], P('segment', None, 'band')
- weight_grad: float32 [8, 2, 2304, 256], P('segment', None, 'band')
All inputs are finite; a program needn't handle non-finite values.
Results may differ from a plain program's by a relative error of at most 0.02.
Values may be sent and summed in bfloat16 or wider, within the bound.
A program may use at most 64 MiB of HBM per device.

v0:
```python
import jax
import jax.numpy as jnp
from jax import lax
from jax.sharding import PartitionSpec as P


def with_halo(value, sides, width):
    for axis, dim in sides:
        count, length = (lax.axis_size(axis), value.shape[dim])
        up = [(i, (i + 1) % count) for i in range(count - 1)]
        down = [(j, i) for i, j in up]
        last = lax.slice_in_dim(value, length - width, length, axis=dim)
        initial = lax.slice_in_dim(value, 0, width, axis=dim)
        before = lax.ppermute(last, axis, up)
        after = lax.ppermute(initial, axis, down)
        value = jnp.concatenate([before, value, after], axis=dim)
    return value


def from_behind(block, axis, distance):
    devices = range(lax.axis_size(axis))
    route = [(i - distance, i) for i in devices if i - distance in devices]
    return lax.ppermute(block, axis, route)


def activate(values):
    return jax.nn.silu(values.astype(jnp.float32)).astype(jnp.bfloat16)


def silu_slope(values):
    sigmoid = jax.nn.sigmoid(values)
    return sigmoid * (1.0 + values * (1.0 - sigmoid))


def gather_taps(rowpadded, flipped):
    height = rowpadded.shape[0] - 2
    across = rowpadded.shape[1]
    padded = jnp.pad(rowpadded, ((0, 0), (1, 1), (0, 0)))
    pieces = []
    for first in range(3):
        for second in range(3):
            if flipped:
                row_start, col_start = (2 - first, 2 - second)
            else:
                row_start, col_start = (first, second)
            pieces.append(padded[row_start : row_start + height, col_start : col_start + across, :])
    return jnp.concatenate(pieces, -1).reshape(height * across, -1)


def apply_taps(taps_matrix, weight):
    return jnp.dot(taps_matrix, weight, preferred_element_type=jnp.float32)


def flip_weight(weight, channels):
    return weight.reshape(9, channels, channels).transpose(0, 2, 1).reshape(9 * channels, channels)


def correlate(taps_matrix, grads):
    return lax.dot_general(
        taps_matrix, grads, (((0,), (0,)), ((), ())), preferred_element_type=jnp.float32
    )


def advance_exchange(state, weight_f, weight_g):
    first_in, second_in = (state[0], state[1])
    shape = first_in.shape
    rim_f = with_halo(activate(second_in), (("band", 0),), 1)
    first_out = (
        first_in.astype(jnp.float32)
        + apply_taps(gather_taps(rim_f, False), weight_f).reshape(shape)
    ).astype(jnp.bfloat16)
    rim_g = with_halo(activate(first_out), (("band", 0),), 1)
    second_out = (
        second_in.astype(jnp.float32)
        + apply_taps(gather_taps(rim_g, False), weight_g).reshape(shape)
    ).astype(jnp.bfloat16)
    return jnp.stack([first_out, second_out])


def invert_exchange(outputs, grads, weight_f, weight_g, flipped_f, flipped_g):
    first_out, second_out = (outputs[0], outputs[1])
    first_grad, second_grad = (grads[0], grads[1])
    shape = first_out.shape
    channels = shape[2]
    act_rim, grad_rim = (
        with_halo(activate(first_out), (("band", 0),), 1),
        with_halo(second_grad, (("band", 0),), 1),
    )
    taps_g = gather_taps(act_rim, False)
    second_in = (
        second_out.astype(jnp.float32) - apply_taps(taps_g, weight_g).reshape(shape)
    ).astype(jnp.bfloat16)
    back_g = apply_taps(gather_taps(grad_rim, True), flipped_g).reshape(shape)
    first_back = (
        first_grad.astype(jnp.float32) + silu_slope(first_out.astype(jnp.float32)) * back_g
    ).astype(jnp.bfloat16)
    act_rim_f, back_rim = (
        with_halo(activate(second_in), (("band", 0),), 1),
        with_halo(first_back, (("band", 0),), 1),
    )
    taps_f = gather_taps(act_rim_f, False)
    first_in = (first_out.astype(jnp.float32) - apply_taps(taps_f, weight_f).reshape(shape)).astype(
        jnp.bfloat16
    )
    back_f = apply_taps(gather_taps(back_rim, True), flipped_f).reshape(shape)
    second_back = (
        second_grad.astype(jnp.float32) + silu_slope(second_in.astype(jnp.float32)) * back_f
    ).astype(jnp.bfloat16)
    wgrad = jnp.stack(
        [
            correlate(taps_f, first_back.reshape(-1, channels)),
            correlate(taps_g, second_grad.reshape(-1, channels)),
        ]
    )
    return (jnp.stack([first_in, second_in]), jnp.stack([first_back, second_back]), wgrad)


def local(forward_state, returning_state, returning_grad, weights, fresh_input, loss_grad):
    segment_index = lax.axis_index("segment")
    last_segment = lax.axis_size("segment") - 1
    weight_f = weights[0, 0]
    weight_g = weights[0, 1]
    channels = weight_f.shape[1]
    flipped_f = flip_weight(weight_f, channels)
    flipped_g = flip_weight(weight_g, channels)
    state = forward_state[0]
    outputs = returning_state[0]
    grads = returning_grad[0]
    totals = jnp.zeros((2, 9 * channels // lax.axis_size("band"), channels), jnp.float32)
    for tick_index in range(fresh_input.shape[0]):
        advanced = advance_exchange(state, weight_f, weight_g)
        inverted, backed, wgrad = invert_exchange(
            outputs, grads, weight_f, weight_g, flipped_f, flipped_g
        )
        totals = totals + lax.psum_scatter(
            wgrad.astype(jnp.bfloat16), "band", scatter_dimension=1, tiled=True
        ).astype(jnp.float32)
        sent = from_behind(advanced, "segment", 1)
        state = jnp.where(segment_index == 0, fresh_input[tick_index], sent)
        came_state, came_grad = from_behind((inverted, backed), "segment", -1)
        at_end = segment_index == last_segment
        outputs = jnp.where(at_end, advanced, came_state)
        grads = jnp.where(at_end, loss_grad[tick_index], came_grad)
    return (state[None], outputs[None], grads[None], totals[None])


def solution(mesh):
    return jax.shard_map(
        local,
        mesh=mesh,
        in_specs=(
            P("segment", None, "band", None, None),
            P("segment", None, "band", None, None),
            P("segment", None, "band", None, None),
            P("segment", None, None, None),
            P(None, None, "band", None, None),
            P(None, None, "band", None, None),
        ),
        out_specs=(
            P("segment", None, "band", None, None),
            P("segment", None, "band", None, None),
            P("segment", None, "band", None, None),
            P("segment", None, "band", None),
        ),
        check_vma=False,
    )
```

profile of v0, /device:TPU:9, one launch (start us, length us, event | category | flops | bytes accessed | tf_op | source)
XLA Modules:
  0.0 182.7 jit_solution(14614851829108012925)
XLA Ops:
  8.0 3.7 %collective-permute-start.20 = (bf16[1,64,256]{2,1,0:T(8,128)(2,1)S(1)}, bf16[1,64,256]{2,1,0:T(8,128)(2,1)S(1)}, u32[]{:S(2)}, u32[]{:S(2)}) collective-permute-start(bf16[1,64,256]{2,1,0:T(8,128)(2,1)S(1)} %get-tuple-element.14), channel_id=1, source_target_pairs={{0,1},{1,2},{2,3},{4,5},{5,6},{6,7},{8,9},{9,10},{10,11},{12,13},{... | collective-permute-start | bytes 98312 | tf_op jit(solution)/shard_map/ppermute | solution.py:14
  11.7 1.9 %collective-permute-start.21 = (bf16[1,64,256]{2,1,0:T(8,128)(2,1)S(1)}, bf16[1,64,256]{2,1,0:T(8,128)(2,1)S(1)}, u32[]{:S(2)}, u32[]{:S(2)}) collective-permute-start(bf16[1,64,256]{2,1,0:T(8,128)(2,1)S(1)} %get-tuple-element.15), channel_id=1, source_target_pairs={{1,0},{2,1},{3,2},{5,4},{6,5},{7,6},{9,8},{10,9},{11,10},{13,12},{... | collective-permute-start | bytes 98312 | tf_op jit(solution)/shard_map/ppermute | solution.py:15
  14.7 3.6 %collective-permute-start = (bf16[1,64,256]{2,1,0:T(8,128)(2,1)S(1)}, bf16[1,64,256]{2,1,0:T(8,128)(2,1)S(1)}, u32[]{:S(2)}, u32[]{:S(2)}) collective-permute-start(bf16[1,64,256]{2,1,0:T(8,128)(2,1)S(1)} %get-tuple-element.38), channel_id=1, source_target_pairs={{0,1},{1,2},{2,3},{4,5},{5,6},{6,7},{8,9},{9,10},{10,11},{12,13},{... | collective-permute-start | bytes 98312 | tf_op jit(solution)/shard_map/ppermute | solution.py:14
  18.4 1.9 %collective-permute-start.1 = (bf16[1,64,256]{2,1,0:T(8,128)(2,1)S(1)}, bf16[1,64,256]{2,1,0:T(8,128)(2,1)S(1)}, u32[]{:S(2)}, u32[]{:S(2)}) collective-permute-start(bf16[1,64,256]{2,1,0:T(8,128)(2,1)S(1)} %get-tuple-element.39), channel_id=1, source_target_pairs={{1,0},{2,1},{3,2},{5,4},{6,5},{7,6},{9,8},{10,9},{11,10},{13,12},{... | collective-permute-start | bytes 98312 | tf_op jit(solution)/shard_map/ppermute | solution.py:15
  22.0 3.8 %collective-permute-start.10 = (bf16[1,64,256]{2,1,0:T(8,128)(2,1)}, bf16[1,64,256]{2,1,0:T(8,128)(2,1)S(1)}, u32[]{:S(2)}, u32[]{:S(2)}) collective-permute-start(bf16[1,64,256]{2,1,0:T(8,128)(2,1)} %get-tuple-element.30), channel_id=1, source_target_pairs={{0,1},{1,2},{2,3},{4,5},{5,6},{6,7},{8,9},{9,10},{10,11},{12,13},{... | collective-permute-start | bytes 98312 | tf_op jit(solution)/shard_map/ppermute | solution.py:14
  36.6 3.8 %collective-permute-start.2 = (bf16[1,64,256]{2,1,0:T(8,128)(2,1)S(1)}, bf16[1,64,256]{2,1,0:T(8,128)(2,1)S(1)}, u32[]{:S(2)}, u32[]{:S(2)}) collective-permute-start(bf16[1,64,256]{2,1,0:T(8,128)(2,1)S(1)} %get-tuple-element.36), channel_id=1, source_target_pairs={{0,1},{1,2},{2,3},{4,5},{5,6},{6,7},{8,9},{9,10},{10,11},{12,13},{... | collective-permute-start | bytes 98312 | tf_op jit(solution)/shard_map/ppermute | solution.py:14
  40.4 1.9 %collective-permute-start.3 = (bf16[1,64,256]{2,1,0:T(8,128)(2,1)S(1)}, bf16[1,64,256]{2,1,0:T(8,128)(2,1)S(1)}, u32[]{:S(2)}, u32[]{:S(2)}) collective-permute-start(bf16[1,64,256]{2,1,0:T(8,128)(2,1)S(1)} %get-tuple-element.37), channel_id=1, source_target_pairs={{1,0},{2,1},{3,2},{5,4},{6,5},{7,6},{9,8},{10,9},{11,10},{13,12},{... | collective-permute-start | bytes 98312 | tf_op jit(solution)/shard_map/ppermute | solution.py:15
  43.9 3.6 %collective-permute-start.12 = (bf16[1,64,256]{2,1,0:T(8,128)(2,1)S(1)}, bf16[1,64,256]{2,1,0:T(8,128)(2,1)S(1)}, u32[]{:S(2)}, u32[]{:S(2)}) collective-permute-start(bf16[1,64,256]{2,1,0:T(8,128)(2,1)S(1)} %get-tuple-element.28), channel_id=1, source_target_pairs={{0,1},{1,2},{2,3},{4,5},{5,6},{6,7},{8,9},{9,10},{10,11},{12,13},{... | collective-permute-start | bytes 98312 | tf_op jit(solution)/shard_map/ppermute | solution.py:14
  47.5 1.9 %collective-permute-start.13 = (bf16[1,64,256]{2,1,0:T(8,128)(2,1)S(1)}, bf16[1,64,256]{2,1,0:T(8,128)(2,1)S(1)}, u32[]{:S(2)}, u32[]{:S(2)}) collective-permute-start(bf16[1,64,256]{2,1,0:T(8,128)(2,1)S(1)} %get-tuple-element.29), channel_id=1, source_target_pairs={{1,0},{2,1},{3,2},{5,4},{6,5},{7,6},{9,8},{10,9},{11,10},{13,12},{... | collective-permute-start | bytes 98312 | tf_op jit(solution)/shard_map/ppermute | solution.py:15
  50.3 3.6 %collective-permute-start.22 = (bf16[1,64,256]{2,1,0:T(8,128)(2,1)S(1)}, bf16[1,64,256]{2,1,0:T(8,128)(2,1)S(1)}, u32[]{:S(2)}, u32[]{:S(2)}) collective-permute-start(bf16[1,64,256]{2,1,0:T(8,128)(2,1)S(1)} %get-tuple-element.22), channel_id=1, source_target_pairs={{0,1},{1,2},{2,3},{4,5},{5,6},{6,7},{8,9},{9,10},{10,11},{12,13},{... | collective-permute-start | bytes 98312 | tf_op jit(solution)/shard_map/ppermute | solution.py:14
  54.8 1.9 %collective-permute-start.23 = (bf16[1,64,256]{2,1,0:T(8,128)(2,1)S(1)}, bf16[1,64,256]{2,1,0:T(8,128)(2,1)S(1)}, u32[]{:S(2)}, u32[]{:S(2)}) collective-permute-start(bf16[1,64,256]{2,1,0:T(8,128)(2,1)S(1)} %get-tuple-element.23), channel_id=1, source_target_pairs={{1,0},{2,1},{3,2},{5,4},{6,5},{7,6},{9,8},{10,9},{11,10},{13,12},{... | collective-permute-start | bytes 98312 | tf_op jit(solution)/shard_map/ppermute | solution.py:15
  61.2 3.0 %collective-permute-start.14 = (bf16[2,8,64,256]{3,2,1,0:T(8,128)(2,1)}, bf16[2,8,64,256]{3,2,1,0:T(8,128)(2,1)}, u32[]{:S(2)}, u32[]{:S(2)}) collective-permute-start(bf16[2,8,64,256]{3,2,1,0:T(8,128)(2,1)} %pad_maximum_fusion.4), channel_id=1, source_target_pairs={{4,0},{8,4},{12,8},{16,12},{20,16},{24,20},{28,24},{5,1},{9,5},{13... | collective-permute-start | bytes 1572872 | tf_op jit(solution)/shard_map/ppermute | solution.py:23
  68.4 2.3 %collective-permute-start.24 = (bf16[2,8,64,256]{3,2,1,0:T(8,128)(2,1)S(1)}, bf16[2,8,64,256]{3,2,1,0:T(8,128)(2,1)S(1)}, u32[]{:S(2)}, u32[]{:S(2)}) collective-permute-start(bf16[2,8,64,256]{3,2,1,0:T(8,128)(2,1)S(1)} %pad_maximum_fusion.6), channel_id=1, source_target_pairs={{4,0},{8,4},{12,8},{16,12},{20,16},{24,20},{28,24},{5,1},{9,5},{13... | collective-permute-start | bytes 1572872 | tf_op jit(solution)/shard_map/ppermute | solution.py:23
  71.6 5.6 %collective-permute-done.14 = bf16[2,8,64,256]{3,2,1,0:T(8,128)(2,1)} collective-permute-done((bf16[2,8,64,256]{3,2,1,0:T(8,128)(2,1)}, bf16[2,8,64,256]{3,2,1,0:T(8,128)(2,1)}, u32[]{:S(2)}, u32[]{:S(2)}) %collective-permute-start.14) | collective-permute-done | bytes 524320 | tf_op jit(solution)/shard_map/ppermute | solution.py:23
  77.2 2.0 %broadcast_select_fusion = (bf16[2,8,64,256]{3,2,1,0:T(8,128)(2,1)S(1)}, bf16[2,8,64,256]{3,2,1,0:T(8,128)(2,1)}) fusion(bf16[2,8,64,256]{3,2,1,0:T(8,128)(2,1)} %collective-permute-done.14, pred[]{:T(512)S(6)} %eq.9, bf16[1,8,64,256]{3,2,1,0:T(8,128)(2,1)S(1)} %fusion.36, bf16[1,8,64,256]{3,2,1,0:T(8,128)(2,1)S(1)} %bitcast.224), kind=kLoop, calls=%fused_computation.131 | loop fusion | flops 524288 | bytes 2097153 | tf_op jit(solution)/shard_map/jit(_where)/select_n | solution.py:142
  79.4 4.6 %collective-permute-start.15 = (bf16[1,64,256]{2,1,0:T(8,128)(2,1)S(1)}, bf16[1,64,256]{2,1,0:T(8,128)(2,1)S(1)}, u32[]{:S(2)}, u32[]{:S(2)}) collective-permute-start(bf16[1,64,256]{2,1,0:T(8,128)(2,1)S(1)} %get-tuple-element.26), channel_id=1, source_target_pairs={{0,1},{1,2},{2,3},{4,5},{5,6},{6,7},{8,9},{9,10},{10,11},{12,13},{... | collective-permute-start | bytes 98312 | tf_op jit(solution)/shard_map/ppermute | solution.py:14
  84.0 1.9 %collective-permute-start.16 = (bf16[1,64,256]{2,1,0:T(8,128)(2,1)S(1)}, bf16[1,64,256]{2,1,0:T(8,128)(2,1)S(1)}, u32[]{:S(2)}, u32[]{:S(2)}) collective-permute-start(bf16[1,64,256]{2,1,0:T(8,128)(2,1)S(1)} %get-tuple-element.27), channel_id=1, source_target_pairs={{1,0},{2,1},{3,2},{5,4},{6,5},{7,6},{9,8},{10,9},{11,10},{13,12},{... | collective-permute-start | bytes 98312 | tf_op jit(solution)/shard_map/ppermute | solution.py:15
  87.3 3.7 %collective-permute-start.4 = (bf16[2,8,64,256]{3,2,1,0:T(8,128)(2,1)}, bf16[2,8,64,256]{3,2,1,0:T(8,128)(2,1)}, u32[]{:S(2)}, u32[]{:S(2)}) collective-permute-start(bf16[2,8,64,256]{3,2,1,0:T(8,128)(2,1)} %get-tuple-element.19), channel_id=1, source_target_pairs={{0,4},{4,8},{8,12},{12,16},{16,20},{20,24},{24,28},{1,5},{5,9},{9,... | collective-permute-start | bytes 1572872 | tf_op jit(solution)/shard_map/ppermute | solution.py:23
  91.0 4.2 %collective-permute-start.25 = (bf16[1,64,256]{2,1,0:T(8,128)(2,1)S(1)}, bf16[1,64,256]{2,1,0:T(8,128)(2,1)S(1)}, u32[]{:S(2)}, u32[]{:S(2)}) collective-permute-start(bf16[1,64,256]{2,1,0:T(8,128)(2,1)S(1)} %get-tuple-element.12), channel_id=1, source_target_pairs={{0,1},{1,2},{2,3},{4,5},{5,6},{6,7},{8,9},{9,10},{10,11},{12,13},{... | collective-permute-start | bytes 98312 | tf_op jit(solution)/shard_map/ppermute | solution.py:14
  95.2 1.9 %collective-permute-start.26 = (bf16[1,64,256]{2,1,0:T(8,128)(2,1)S(1)}, bf16[1,64,256]{2,1,0:T(8,128)(2,1)S(1)}, u32[]{:S(2)}, u32[]{:S(2)}) collective-permute-start(bf16[1,64,256]{2,1,0:T(8,128)(2,1)S(1)} %get-tuple-element.13), channel_id=1, source_target_pairs={{1,0},{2,1},{3,2},{5,4},{6,5},{7,6},{9,8},{10,9},{11,10},{13,12},{... | collective-permute-start | bytes 98312 | tf_op jit(solution)/shard_map/ppermute | solution.py:15
  98.7 3.6 %collective-permute-start.17 = (bf16[1,64,256]{2,1,0:T(8,128)(2,1)S(1)}, bf16[1,64,256]{2,1,0:T(8,128)(2,1)S(1)}, u32[]{:S(2)}, u32[]{:S(2)}) collective-permute-start(bf16[1,64,256]{2,1,0:T(8,128)(2,1)S(1)} %get-tuple-element.24), channel_id=1, source_target_pairs={{0,1},{1,2},{2,3},{4,5},{5,6},{6,7},{8,9},{9,10},{10,11},{12,13},{... | collective-permute-start | bytes 98312 | tf_op jit(solution)/shard_map/ppermute | solution.py:14
  106.5 3.6 %collective-permute-start.27 = (bf16[1,64,256]{2,1,0:T(8,128)(2,1)S(1)}, bf16[1,64,256]{2,1,0:T(8,128)(2,1)S(1)}, u32[]{:S(2)}, u32[]{:S(2)}) collective-permute-start(bf16[1,64,256]{2,1,0:T(8,128)(2,1)S(1)} %get-tuple-element.20), channel_id=1, source_target_pairs={{0,1},{1,2},{2,3},{4,5},{5,6},{6,7},{8,9},{9,10},{10,11},{12,13},{... | collective-permute-start | bytes 98312 | tf_op jit(solution)/shard_map/ppermute | solution.py:14
  110.2 1.9 %collective-permute-start.28 = (bf16[1,64,256]{2,1,0:T(8,128)(2,1)S(1)}, bf16[1,64,256]{2,1,0:T(8,128)(2,1)S(1)}, u32[]{:S(2)}, u32[]{:S(2)}) collective-permute-start(bf16[1,64,256]{2,1,0:T(8,128)(2,1)S(1)} %get-tuple-element.21), channel_id=1, source_target_pairs={{1,0},{2,1},{3,2},{5,4},{6,5},{7,6},{9,8},{10,9},{11,10},{13,12},{... | collective-permute-start | bytes 98312 | tf_op jit(solution)/shard_map/ppermute | solution.py:15
  115.2 2.1 %collective-permute-start.19 = (bf16[2,8,64,256]{3,2,1,0:T(8,128)(2,1)}, bf16[2,8,64,256]{3,2,1,0:T(8,128)(2,1)}, u32[]{:S(2)}, u32[]{:S(2)}) collective-permute-start(bf16[2,8,64,256]{3,2,1,0:T(8,128)(2,1)} %pad_maximum_fusion.5), channel_id=1, source_target_pairs={{4,0},{8,4},{12,8},{16,12},{20,16},{24,20},{28,24},{5,1},{9,5},{13... | collective-permute-start | bytes 1572872 | tf_op jit(solution)/shard_map/ppermute | solution.py:23
  129.1 3.9 %collective-permute-start.5 = (bf16[1,64,256]{2,1,0:T(8,128)(2,1)S(1)}, bf16[1,64,256]{2,1,0:T(8,128)(2,1)S(1)}, u32[]{:S(2)}, u32[]{:S(2)}) collective-permute-start(bf16[1,64,256]{2,1,0:T(8,128)(2,1)S(1)} %get-tuple-element.34), channel_id=1, source_target_pairs={{0,1},{1,2},{2,3},{4,5},{5,6},{6,7},{8,9},{9,10},{10,11},{12,13},{... | collective-permute-start | bytes 98312 | tf_op jit(solution)/shard_map/ppermute | solution.py:14
  135.0 3.6 %fusion.85 = bf16[1,8,64,256]{3,2,1,0:T(8,128)(2,1)} fusion(bf16[8,64,2304]{2,1,0:T(8,128)(2,1)} %slice_dynamic-update-slice_fusion, bf16[2304,256,1]{1,0,2:T(8,128)(2,1)} %bitcast.220, bf16[8,64,256]{2,1,0:T(8,128)(2,1)} %copy-done.11, bf16[2,8,64,256]{3,2,1,0:T(8,128)(2,1)S(1)} %bitcast_select_fusion), kind=kOutput, calls=%fused_computation.132 | convolution fusion | flops 605552640 | bytes 4325376 | tf_op jit(solution)/shard_map/dot_general | solution.py:51
  140.8 3.6 %collective-permute-start.7 = (bf16[1,64,256]{2,1,0:T(8,128)(2,1)S(1)}, bf16[1,64,256]{2,1,0:T(8,128)(2,1)S(1)}, u32[]{:S(2)}, u32[]{:S(2)}) collective-permute-start(bf16[1,64,256]{2,1,0:T(8,128)(2,1)S(1)} %get-tuple-element.32), channel_id=1, source_target_pairs={{0,1},{1,2},{2,3},{4,5},{5,6},{6,7},{8,9},{9,10},{10,11},{12,13},{... | collective-permute-start | bytes 98312 | tf_op jit(solution)/shard_map/ppermute | solution.py:14
  146.4 3.8 %collective-permute-start.29 = (bf16[2,8,64,256]{3,2,1,0:T(8,128)(2,1)S(1)}, bf16[2,8,64,256]{3,2,1,0:T(8,128)(2,1)S(1)}, u32[]{:S(2)}, u32[]{:S(2)}) collective-permute-start(bf16[2,8,64,256]{3,2,1,0:T(8,128)(2,1)S(1)} %pad_maximum_fusion.7), channel_id=1, source_target_pairs={{4,0},{8,4},{12,8},{16,12},{20,16},{24,20},{28,24},{5,1},{9,5},{13... | collective-permute-start | bytes 1572872 | tf_op jit(solution)/shard_map/ppermute | solution.py:23
  151.6 2.1 %select_bitcast_fusion = (bf16[1,2,8,64,256]{4,3,2,1,0:T(8,128)(2,1)}, bf16[2,8,64,256]{3,2,1,0:T(8,128)(2,1)S(1)}) fusion(bf16[2,8,64,256]{3,2,1,0:T(8,128)(2,1)} %collective-permute-done.19, pred[]{:T(512)S(6)} %eq.9, bf16[1,8,64,256]{3,2,1,0:T(8,128)(2,1)S(1)} %fusion.33, bf16[1,8,64,256]{3,2,1,0:T(8,128)(2,1)S(1)} %get-tuple-element.6), kind=kLoop, calls=%fused_computation.130 | loop fusion | flops 524288 | bytes 2097153 | tf_op jit(solution)/shard_map/broadcast_in_dim | solution.py:144
  153.7 2.5 %collective-permute-start.9 = (bf16[2,8,64,256]{3,2,1,0:T(8,128)(2,1)S(1)}, bf16[2,8,64,256]{3,2,1,0:T(8,128)(2,1)S(1)}, u32[]{:S(2)}, u32[]{:S(2)}) collective-permute-start(bf16[2,8,64,256]{3,2,1,0:T(8,128)(2,1)S(1)} %get-tuple-element.17), channel_id=1, source_target_pairs={{0,4},{4,8},{8,12},{12,16},{16,20},{20,24},{24,28},{1,5},{5,9},{9,... | collective-permute-start | bytes 1572872 | tf_op jit(solution)/shard_map/ppermute | solution.py:23
  156.2 15.6 %collective-permute-done.29 = bf16[2,8,64,256]{3,2,1,0:T(8,128)(2,1)S(1)} collective-permute-done((bf16[2,8,64,256]{3,2,1,0:T(8,128)(2,1)S(1)}, bf16[2,8,64,256]{3,2,1,0:T(8,128)(2,1)S(1)}, u32[]{:S(2)}, u32[]{:S(2)}) %collective-permute-start.29) | collective-permute-done | bytes 524320 | tf_op jit(solution)/shard_map/ppermute | solution.py:23
  173.5 2.4 %add_bitcast_fusion = f32[1,2,576,256]{3,2,1,0:T(8,128)} fusion(bf16[2,576,256]{2,1,0:T(8,128)(2,1)} %reduce-scatter.5.cloned.1.call-done, bf16[2,576,256]{2,1,0:T(8,128)(2,1)} %reduce-scatter.3.cloned.1.call-done), kind=kLoop, calls=%fused_computation.42 | loop fusion | flops 884736 | bytes 2359296 | tf_op jit(solution)/shard_map/broadcast_in_dim | solution.py:144
  (254 shorter events, 57.1 us)
Async XLA Ops:
  7.2 166.4 %reduce-scatter.3.cloned.1.call-start = ((), (), s32[]{:S(2)}) async-start(), calls=%async_computation.2 | async-start | bytes 2949120 | tf_op jit(solution)/shard_map/reduce_scatter | solution.py:135
  8.0 23.5 %collective-permute-start.20 = (bf16[1,64,256]{2,1,0:T(8,128)(2,1)S(1)}, bf16[1,64,256]{2,1,0:T(8,128)(2,1)S(1)}, u32[]{:S(2)}, u32[]{:S(2)}) collective-permute-start(bf16[1,64,256]{2,1,0:T(8,128)(2,1)S(1)} %get-tuple-element.14), channel_id=1, source_target_pairs={{0,1},{1,2},{2,3},{4,5},{5,6},{6,7},{8,9},{9,10},{10,11},{12,13},{... | collective-permute-start | bytes 98312 | tf_op jit(solution)/shard_map/ppermute | solution.py:14
  11.7 21.7 %collective-permute-start.21 = (bf16[1,64,256]{2,1,0:T(8,128)(2,1)S(1)}, bf16[1,64,256]{2,1,0:T(8,128)(2,1)S(1)}, u32[]{:S(2)}, u32[]{:S(2)}) collective-permute-start(bf16[1,64,256]{2,1,0:T(8,128)(2,1)S(1)} %get-tuple-element.15), channel_id=1, source_target_pairs={{1,0},{2,1},{3,2},{5,4},{6,5},{7,6},{9,8},{10,9},{11,10},{13,12},{... | collective-permute-start | bytes 98312 | tf_op jit(solution)/shard_map/ppermute | solution.py:15
  14.7 19.2 %collective-permute-start = (bf16[1,64,256]{2,1,0:T(8,128)(2,1)S(1)}, bf16[1,64,256]{2,1,0:T(8,128)(2,1)S(1)}, u32[]{:S(2)}, u32[]{:S(2)}) collective-permute-start(bf16[1,64,256]{2,1,0:T(8,128)(2,1)S(1)} %get-tuple-element.38), channel_id=1, source_target_pairs={{0,1},{1,2},{2,3},{4,5},{5,6},{6,7},{8,9},{9,10},{10,11},{12,13},{... | collective-permute-start | bytes 98312 | tf_op jit(solution)/shard_map/ppermute | solution.py:14
  18.4 15.6 %collective-permute-start.1 = (bf16[1,64,256]{2,1,0:T(8,128)(2,1)S(1)}, bf16[1,64,256]{2,1,0:T(8,128)(2,1)S(1)}, u32[]{:S(2)}, u32[]{:S(2)}) collective-permute-start(bf16[1,64,256]{2,1,0:T(8,128)(2,1)S(1)} %get-tuple-element.39), channel_id=1, source_target_pairs={{1,0},{2,1},{3,2},{5,4},{6,5},{7,6},{9,8},{10,9},{11,10},{13,12},{... | collective-permute-start | bytes 98312 | tf_op jit(solution)/shard_map/ppermute | solution.py:15
  22.0 20.3 %collective-permute-start.10 = (bf16[1,64,256]{2,1,0:T(8,128)(2,1)}, bf16[1,64,256]{2,1,0:T(8,128)(2,1)S(1)}, u32[]{:S(2)}, u32[]{:S(2)}) collective-permute-start(bf16[1,64,256]{2,1,0:T(8,128)(2,1)} %get-tuple-element.30), channel_id=1, source_target_pairs={{0,1},{1,2},{2,3},{4,5},{5,6},{6,7},{8,9},{9,10},{10,11},{12,13},{... | collective-permute-start | bytes 98312 | tf_op jit(solution)/shard_map/ppermute | solution.py:14
  31.5 10.9 %collective-permute-start.11 = (bf16[1,64,256]{2,1,0:T(8,128)(2,1)S(1)}, bf16[1,64,256]{2,1,0:T(8,128)(2,1)S(1)}, u32[]{:S(2)}, u32[]{:S(2)}) collective-permute-start(bf16[1,64,256]{2,1,0:T(8,128)(2,1)S(1)} %get-tuple-element.31), channel_id=1, source_target_pairs={{1,0},{2,1},{3,2},{5,4},{6,5},{7,6},{9,8},{10,9},{11,10},{13,12},{... | collective-permute-start | bytes 98312 | tf_op jit(solution)/shard_map/ppermute | solution.py:15
  36.6 22.4 %collective-permute-start.2 = (bf16[1,64,256]{2,1,0:T(8,128)(2,1)S(1)}, bf16[1,64,256]{2,1,0:T(8,128)(2,1)S(1)}, u32[]{:S(2)}, u32[]{:S(2)}) collective-permute-start(bf16[1,64,256]{2,1,0:T(8,128)(2,1)S(1)} %get-tuple-element.36), channel_id=1, source_target_pairs={{0,1},{1,2},{2,3},{4,5},{5,6},{6,7},{8,9},{9,10},{10,11},{12,13},{... | collective-permute-start | bytes 98312 | tf_op jit(solution)/shard_map/ppermute | solution.py:14
  40.4 18.6 %collective-permute-start.3 = (bf16[1,64,256]{2,1,0:T(8,128)(2,1)S(1)}, bf16[1,64,256]{2,1,0:T(8,128)(2,1)S(1)}, u32[]{:S(2)}, u32[]{:S(2)}) collective-permute-start(bf16[1,64,256]{2,1,0:T(8,128)(2,1)S(1)} %get-tuple-element.37), channel_id=1, source_target_pairs={{1,0},{2,1},{3,2},{5,4},{6,5},{7,6},{9,8},{10,9},{11,10},{13,12},{... | collective-permute-start | bytes 98312 | tf_op jit(solution)/shard_map/ppermute | solution.py:15
  43.9 11.0 %collective-permute-start.12 = (bf16[1,64,256]{2,1,0:T(8,128)(2,1)S(1)}, bf16[1,64,256]{2,1,0:T(8,128)(2,1)S(1)}, u32[]{:S(2)}, u32[]{:S(2)}) collective-permute-start(bf16[1,64,256]{2,1,0:T(8,128)(2,1)S(1)} %get-tuple-element.28), channel_id=1, source_target_pairs={{0,1},{1,2},{2,3},{4,5},{5,6},{6,7},{8,9},{9,10},{10,11},{12,13},{... | collective-permute-start | bytes 98312 | tf_op jit(solution)/shard_map/ppermute | solution.py:14
  47.5 9.2 %collective-permute-start.13 = (bf16[1,64,256]{2,1,0:T(8,128)(2,1)S(1)}, bf16[1,64,256]{2,1,0:T(8,128)(2,1)S(1)}, u32[]{:S(2)}, u32[]{:S(2)}) collective-permute-start(bf16[1,64,256]{2,1,0:T(8,128)(2,1)S(1)} %get-tuple-element.29), channel_id=1, source_target_pairs={{1,0},{2,1},{3,2},{5,4},{6,5},{7,6},{9,8},{10,9},{11,10},{13,12},{... | collective-permute-start | bytes 98312 | tf_op jit(solution)/shard_map/ppermute | solution.py:15
  50.3 15.6 %collective-permute-start.22 = (bf16[1,64,256]{2,1,0:T(8,128)(2,1)S(1)}, bf16[1,64,256]{2,1,0:T(8,128)(2,1)S(1)}, u32[]{:S(2)}, u32[]{:S(2)}) collective-permute-start(bf16[1,64,256]{2,1,0:T(8,128)(2,1)S(1)} %get-tuple-element.22), channel_id=1, source_target_pairs={{0,1},{1,2},{2,3},{4,5},{5,6},{6,7},{8,9},{9,10},{10,11},{12,13},{... | collective-permute-start | bytes 98312 | tf_op jit(solution)/shard_map/ppermute | solution.py:14
  54.8 11.1 %collective-permute-start.23 = (bf16[1,64,256]{2,1,0:T(8,128)(2,1)S(1)}, bf16[1,64,256]{2,1,0:T(8,128)(2,1)S(1)}, u32[]{:S(2)}, u32[]{:S(2)}) collective-permute-start(bf16[1,64,256]{2,1,0:T(8,128)(2,1)S(1)} %get-tuple-element.23), channel_id=1, source_target_pairs={{1,0},{2,1},{3,2},{5,4},{6,5},{7,6},{9,8},{10,9},{11,10},{13,12},{... | collective-permute-start | bytes 98312 | tf_op jit(solution)/shard_map/ppermute | solution.py:15
  61.2 16.0 %collective-permute-start.14 = (bf16[2,8,64,256]{3,2,1,0:T(8,128)(2,1)}, bf16[2,8,64,256]{3,2,1,0:T(8,128)(2,1)}, u32[]{:S(2)}, u32[]{:S(2)}) collective-permute-start(bf16[2,8,64,256]{3,2,1,0:T(8,128)(2,1)} %pad_maximum_fusion.4), channel_id=1, source_target_pairs={{4,0},{8,4},{12,8},{16,12},{20,16},{24,20},{28,24},{5,1},{9,5},{13... | collective-permute-start | bytes 1572872 | tf_op jit(solution)/shard_map/ppermute | solution.py:23
  65.8 107.7 %reduce-scatter.5.cloned.1.call-start = ((), (), s32[]{:S(2)}) async-start(), calls=%async_computation.3 | async-start | bytes 2949120 | tf_op jit(solution)/shard_map/reduce_scatter | solution.py:135
  68.4 18.8 %collective-permute-start.24 = (bf16[2,8,64,256]{3,2,1,0:T(8,128)(2,1)S(1)}, bf16[2,8,64,256]{3,2,1,0:T(8,128)(2,1)S(1)}, u32[]{:S(2)}, u32[]{:S(2)}) collective-permute-start(bf16[2,8,64,256]{3,2,1,0:T(8,128)(2,1)S(1)} %pad_maximum_fusion.6), channel_id=1, source_target_pairs={{4,0},{8,4},{12,8},{16,12},{20,16},{24,20},{28,24},{5,1},{9,5},{13... | collective-permute-start | bytes 1572872 | tf_op jit(solution)/shard_map/ppermute | solution.py:23
  79.4 17.8 %collective-permute-start.15 = (bf16[1,64,256]{2,1,0:T(8,128)(2,1)S(1)}, bf16[1,64,256]{2,1,0:T(8,128)(2,1)S(1)}, u32[]{:S(2)}, u32[]{:S(2)}) collective-permute-start(bf16[1,64,256]{2,1,0:T(8,128)(2,1)S(1)} %get-tuple-element.26), channel_id=1, source_target_pairs={{0,1},{1,2},{2,3},{4,5},{5,6},{6,7},{8,9},{9,10},{10,11},{12,13},{... | collective-permute-start | bytes 98312 | tf_op jit(solution)/shard_map/ppermute | solution.py:14
  84.0 13.2 %collective-permute-start.16 = (bf16[1,64,256]{2,1,0:T(8,128)(2,1)S(1)}, bf16[1,64,256]{2,1,0:T(8,128)(2,1)S(1)}, u32[]{:S(2)}, u32[]{:S(2)}) collective-permute-start(bf16[1,64,256]{2,1,0:T(8,128)(2,1)S(1)} %get-tuple-element.27), channel_id=1, source_target_pairs={{1,0},{2,1},{3,2},{5,4},{6,5},{7,6},{9,8},{10,9},{11,10},{13,12},{... | collective-permute-start | bytes 98312 | tf_op jit(solution)/shard_map/ppermute | solution.py:15
  87.3 39.6 %collective-permute-start.4 = (bf16[2,8,64,256]{3,2,1,0:T(8,128)(2,1)}, bf16[2,8,64,256]{3,2,1,0:T(8,128)(2,1)}, u32[]{:S(2)}, u32[]{:S(2)}) collective-permute-start(bf16[2,8,64,256]{3,2,1,0:T(8,128)(2,1)} %get-tuple-element.19), channel_id=1, source_target_pairs={{0,4},{4,8},{8,12},{12,16},{16,20},{20,24},{24,28},{1,5},{5,9},{9,... | collective-permute-start | bytes 1572872 | tf_op jit(solution)/shard_map/ppermute | solution.py:23
  91.0 13.2 %collective-permute-start.25 = (bf16[1,64,256]{2,1,0:T(8,128)(2,1)S(1)}, bf16[1,64,256]{2,1,0:T(8,128)(2,1)S(1)}, u32[]{:S(2)}, u32[]{:S(2)}) collective-permute-start(bf16[1,64,256]{2,1,0:T(8,128)(2,1)S(1)} %get-tuple-element.12), channel_id=1, source_target_pairs={{0,1},{1,2},{2,3},{4,5},{5,6},{6,7},{8,9},{9,10},{10,11},{12,13},{... | collective-permute-start | bytes 98312 | tf_op jit(solution)/shard_map/ppermute | solution.py:14
  95.2 9.0 %collective-permute-start.26 = (bf16[1,64,256]{2,1,0:T(8,128)(2,1)S(1)}, bf16[1,64,256]{2,1,0:T(8,128)(2,1)S(1)}, u32[]{:S(2)}, u32[]{:S(2)}) collective-permute-start(bf16[1,64,256]{2,1,0:T(8,128)(2,1)S(1)} %get-tuple-element.13), channel_id=1, source_target_pairs={{1,0},{2,1},{3,2},{5,4},{6,5},{7,6},{9,8},{10,9},{11,10},{13,12},{... | collective-permute-start | bytes 98312 | tf_op jit(solution)/shard_map/ppermute | solution.py:15
  98.7 14.2 %collective-permute-start.17 = (bf16[1,64,256]{2,1,0:T(8,128)(2,1)S(1)}, bf16[1,64,256]{2,1,0:T(8,128)(2,1)S(1)}, u32[]{:S(2)}, u32[]{:S(2)}) collective-permute-start(bf16[1,64,256]{2,1,0:T(8,128)(2,1)S(1)} %get-tuple-element.24), channel_id=1, source_target_pairs={{0,1},{1,2},{2,3},{4,5},{5,6},{6,7},{8,9},{9,10},{10,11},{12,13},{... | collective-permute-start | bytes 98312 | tf_op jit(solution)/shard_map/ppermute | solution.py:14
  102.3 10.6 %collective-permute-start.18 = (bf16[1,64,256]{2,1,0:T(8,128)(2,1)S(1)}, bf16[1,64,256]{2,1,0:T(8,128)(2,1)S(1)}, u32[]{:S(2)}, u32[]{:S(2)}) collective-permute-start(bf16[1,64,256]{2,1,0:T(8,128)(2,1)S(1)} %get-tuple-element.25), channel_id=1, source_target_pairs={{1,0},{2,1},{3,2},{5,4},{6,5},{7,6},{9,8},{10,9},{11,10},{13,12},{... | collective-permute-start | bytes 98312 | tf_op jit(solution)/shard_map/ppermute | solution.py:15
  106.5 10.8 %collective-permute-start.27 = (bf16[1,64,256]{2,1,0:T(8,128)(2,1)S(1)}, bf16[1,64,256]{2,1,0:T(8,128)(2,1)S(1)}, u32[]{:S(2)}, u32[]{:S(2)}) collective-permute-start(bf16[1,64,256]{2,1,0:T(8,128)(2,1)S(1)} %get-tuple-element.20), channel_id=1, source_target_pairs={{0,1},{1,2},{2,3},{4,5},{5,6},{6,7},{8,9},{9,10},{10,11},{12,13},{... | collective-permute-start | bytes 98312 | tf_op jit(solution)/shard_map/ppermute | solution.py:14
  110.2 7.2 %collective-permute-start.28 = (bf16[1,64,256]{2,1,0:T(8,128)(2,1)S(1)}, bf16[1,64,256]{2,1,0:T(8,128)(2,1)S(1)}, u32[]{:S(2)}, u32[]{:S(2)}) collective-permute-start(bf16[1,64,256]{2,1,0:T(8,128)(2,1)S(1)} %get-tuple-element.21), channel_id=1, source_target_pairs={{1,0},{2,1},{3,2},{5,4},{6,5},{7,6},{9,8},{10,9},{11,10},{13,12},{... | collective-permute-start | bytes 98312 | tf_op jit(solution)/shard_map/ppermute | solution.py:15
  115.2 36.4 %collective-permute-start.19 = (bf16[2,8,64,256]{3,2,1,0:T(8,128)(2,1)}, bf16[2,8,64,256]{3,2,1,0:T(8,128)(2,1)}, u32[]{:S(2)}, u32[]{:S(2)}) collective-permute-start(bf16[2,8,64,256]{3,2,1,0:T(8,128)(2,1)} %pad_maximum_fusion.5), channel_id=1, source_target_pairs={{4,0},{8,4},{12,8},{16,12},{20,16},{24,20},{28,24},{5,1},{9,5},{13... | collective-permute-start | bytes 1572872 | tf_op jit(solution)/shard_map/ppermute | solution.py:23
  129.1 9.4 %collective-permute-start.5 = (bf16[1,64,256]{2,1,0:T(8,128)(2,1)S(1)}, bf16[1,64,256]{2,1,0:T(8,128)(2,1)S(1)}, u32[]{:S(2)}, u32[]{:S(2)}) collective-permute-start(bf16[1,64,256]{2,1,0:T(8,128)(2,1)S(1)} %get-tuple-element.34), channel_id=1, source_target_pairs={{0,1},{1,2},{2,3},{4,5},{5,6},{6,7},{8,9},{9,10},{10,11},{12,13},{... | collective-permute-start | bytes 98312 | tf_op jit(solution)/shard_map/ppermute | solution.py:14
  133.0 5.5 %collective-permute-start.6 = (bf16[1,64,256]{2,1,0:T(8,128)(2,1)S(1)}, bf16[1,64,256]{2,1,0:T(8,128)(2,1)S(1)}, u32[]{:S(2)}, u32[]{:S(2)}) collective-permute-start(bf16[1,64,256]{2,1,0:T(8,128)(2,1)S(1)} %get-tuple-element.35), channel_id=1, source_target_pairs={{1,0},{2,1},{3,2},{5,4},{6,5},{7,6},{9,8},{10,9},{11,10},{13,12},{... | collective-permute-start | bytes 98312 | tf_op jit(solution)/shard_map/ppermute | solution.py:15
  140.8 9.5 %collective-permute-start.7 = (bf16[1,64,256]{2,1,0:T(8,128)(2,1)S(1)}, bf16[1,64,256]{2,1,0:T(8,128)(2,1)S(1)}, u32[]{:S(2)}, u32[]{:S(2)}) collective-permute-start(bf16[1,64,256]{2,1,0:T(8,128)(2,1)S(1)} %get-tuple-element.32), channel_id=1, source_target_pairs={{0,1},{1,2},{2,3},{4,5},{5,6},{6,7},{8,9},{9,10},{10,11},{12,13},{... | collective-permute-start | bytes 98312 | tf_op jit(solution)/shard_map/ppermute | solution.py:14
  144.4 5.9 %collective-permute-start.8 = (bf16[1,64,256]{2,1,0:T(8,128)(2,1)S(1)}, bf16[1,64,256]{2,1,0:T(8,128)(2,1)S(1)}, u32[]{:S(2)}, u32[]{:S(2)}) collective-permute-start(bf16[1,64,256]{2,1,0:T(8,128)(2,1)S(1)} %get-tuple-element.33), channel_id=1, source_target_pairs={{1,0},{2,1},{3,2},{5,4},{6,5},{7,6},{9,8},{10,9},{11,10},{13,12},{... | collective-permute-start | bytes 98312 | tf_op jit(solution)/shard_map/ppermute | solution.py:15
  146.4 25.4 %collective-permute-start.29 = (bf16[2,8,64,256]{3,2,1,0:T(8,128)(2,1)S(1)}, bf16[2,8,64,256]{3,2,1,0:T(8,128)(2,1)S(1)}, u32[]{:S(2)}, u32[]{:S(2)}) collective-permute-start(bf16[2,8,64,256]{3,2,1,0:T(8,128)(2,1)S(1)} %pad_maximum_fusion.7), channel_id=1, source_target_pairs={{4,0},{8,4},{12,8},{16,12},{20,16},{24,20},{28,24},{5,1},{9,5},{13... | collective-permute-start | bytes 1572872 | tf_op jit(solution)/shard_map/ppermute | solution.py:23
  153.7 19.0 %collective-permute-start.9 = (bf16[2,8,64,256]{3,2,1,0:T(8,128)(2,1)S(1)}, bf16[2,8,64,256]{3,2,1,0:T(8,128)(2,1)S(1)}, u32[]{:S(2)}, u32[]{:S(2)}) collective-permute-start(bf16[2,8,64,256]{3,2,1,0:T(8,128)(2,1)S(1)} %get-tuple-element.17), channel_id=1, source_target_pairs={{0,4},{4,8},{8,12},{12,16},{16,20},{20,24},{24,28},{1,5},{5,9},{9,... | collective-permute-start | bytes 1572872 | tf_op jit(solution)/shard_map/ppermute | solution.py:23
  (25 other events, 174.7 us)
Sparse Core Ops, SparseCore 0:
  66.0 34.2 reduce-scatter.2
  138.7 32.8 reduce-scatter.4
where the time goes:
time: 185 us; the launch traced here: 183 us
  starting transfers between devices  86.4 us (47%)
  waiting for transfers between devices  22.6 us (12%)
  other arithmetic  21.4 us (12%)
  local copies, waits for them, and re-layouts  20.9 us (11%)
  between operations  15.8 us (9%)
  matrix products  15.7 us (8%)
    ppermute x12, starting transfers between devices, with_halo(): before = lax.ppermute(last, axis, up)  45.8 us
    ppermute x12, starting transfers between devices, with_halo(): after = lax.ppermute(initial, axis, down)  23 us
    ppermute x6, waiting for transfers between devices, from_behind(): return lax.ppermute(block, axis, route)  22.5 us
    ppermute x6, starting transfers between devices, from_behind(): return lax.ppermute(block, axis, route)  17.5 us
    unnamed x115, local copies, waits for them, and re-layouts  12.4 us
    dot_general x12, matrix products, apply_taps(): return jnp.dot(taps_matrix, weight, preferred_element_type=jnp.float32)  12.4 us
    broadcast_in_dim x4, other arithmetic, local(): return (state[None], outputs[None], grads[None], totals[None])  6.14 us
  transfers between devices with their start and end apart: 32, of which 3 were waited for; matrix products, arithmetic and copies ran while one was open for 27% of the time, Pallas kernels for 0%

commit v1 on v0

v1 whole, which is shorter than its diff:
```python
import functools

import jax
import jax.numpy as jnp
from jax import lax
from jax.experimental import pallas as pl
from jax.experimental.pallas import tpu as pltpu
from jax.sharding import PartitionSpec as P

MESH = pl.DeviceIdType.MESH
ACT_Q, ACT_OUT, ACT_Y, GRAD2, ACT_IN, BACK1 = range(6)
FWD1, FWD2, RET1, RET2, GRD1, GRD2 = range(6)


def kernel(ticks, segments, bands, width, fwd_in, ret_in, grd_in, weights_in, fresh_in, loss_in,
           fwd_out, ret_out, grd_out, wgrad_out,
           fwd_v, ret_v, grd_v, wts, flipped, stack, halo_src, halo_dst, sent, came, total, total_half, partial,
           in_sem, edge_sem, halo_send, halo_recv, move_send, move_recv, red_send, red_recv):
    seg = lax.axis_index("segment")
    band = lax.axis_index("band")
    pixels = fwd_v.shape[1]
    channels = fwd_v.shape[2]
    triple = 3 * channels
    chunk = partial.shape[2]
    first_seg, last_seg = seg == 0, seg == segments - 1

    loads = [
        pltpu.make_async_copy(fwd_in, fwd_v, in_sem.at[0]),
        pltpu.make_async_copy(ret_in, ret_v, in_sem.at[1]),
        pltpu.make_async_copy(grd_in, grd_v, in_sem.at[2]),
        pltpu.make_async_copy(weights_in.at[0], wts.at[0], in_sem.at[3]),
        pltpu.make_async_copy(weights_in.at[1], wts.at[1], in_sem.at[4]),
    ]
    for load in loads:
        load.start()

    barrier = pltpu.get_barrier_semaphore()
    for step in range(1, bands):
        pl.semaphore_signal(barrier, inc=1, device_id=(seg, lax.rem(band + step, bands)), device_id_type=MESH)

    @pl.when(seg > 0)
    def _():
        pl.semaphore_signal(barrier, inc=1, device_id=(seg - 1, band), device_id_type=MESH)

    @pl.when(seg < segments - 1)
    def _():
        pl.semaphore_signal(barrier, inc=1, device_id=(seg + 1, band), device_id_type=MESH)

    def landing(tick, field):
        if tick < ticks - 1:
            return came.at[tick, field]
        return (fwd_out, ret_out, grd_out)[field // 2].at[field % 2]

    def edge_copies(tick):
        if tick < ticks - 1:
            targets = (came.at[tick, pl.ds(FWD1, 2)], came.at[tick, pl.ds(GRD1, 2)])
        else:
            targets = (fwd_out, grd_out)
        return (
            pltpu.make_async_copy(fresh_in.at[tick], targets[0], edge_sem.at[tick, 0]),
            pltpu.make_async_copy(loss_in.at[tick], targets[1], edge_sem.at[tick, 1]),
        )

    for tick in range(ticks):
        fresh_copy, loss_copy = edge_copies(tick)
        pl.when(first_seg)(fresh_copy.start)
        pl.when(last_seg)(loss_copy.start)

    column = lax.rem(lax.broadcasted_iota(jnp.int32, (pixels, channels), 0), width)
    at_left, at_right = column == 0, column == width - 1

    def fill(field, start, value):
        rows = value.shape[0]
        wide = value.astype(jnp.float32)
        left = jnp.where(at_left[:rows], 0.0, pltpu.roll(wide, 1, 0))
        right = jnp.where(at_right[:rows], 0.0, pltpu.roll(wide, rows - 1, 0))
        stack[field, start:start + rows, 0:channels] = left.astype(jnp.bfloat16)
        stack[field, start:start + rows, channels:2 * channels] = value
        stack[field, start:start + rows, 2 * channels:triple] = right.astype(jnp.bfloat16)

    def halo_copy(tick, field, side):
        return pltpu.make_async_remote_copy(
            src_ref=halo_src.at[tick, field, side], dst_ref=halo_dst.at[tick, field, 1 - side],
            send_sem=halo_send.at[tick, field, side], recv_sem=halo_recv.at[tick, field, 1 - side],
            device_id=(seg, band - 1 if side == 0 else band + 1), device_id_type=MESH)

    def prepare(tick, field, value):
        halo_src[tick, field, 0] = value[:width]
        halo_src[tick, field, 1] = value[pixels - width:]

    def send_halo(tick, field):
        pl.when(band > 0)(halo_copy(tick, field, 0).start)
        pl.when(band < bands - 1)(halo_copy(tick, field, 1).start)

    def take_halo(tick, field):
        zero = jnp.zeros((width, triple), jnp.bfloat16)

        @pl.when(band > 0)
        def _():
            halo_copy(tick, field, 1).wait_recv()
            fill(field, 0, halo_dst[tick, field, 0])

        @pl.when(band == 0)
        def _():
            stack[field, 0:width] = zero

        @pl.when(band < bands - 1)
        def _():
            halo_copy(tick, field, 0).wait_recv()
            fill(field, pixels + width, halo_dst[tick, field, 1])

        @pl.when(band == bands - 1)
        def _():
            stack[field, pixels + width:pixels + 2 * width] = zero

    def apply(field, kernel_ref):
        result = None
        for row in range(3):
            term = jnp.dot(stack[field, row * width:row * width + pixels],
                           kernel_ref[row * triple:(row + 1) * triple],
                           preferred_element_type=jnp.float32)
            result = term if result is None else result + term
        return result

    def correlate(tick, index, field, grads):
        for row in range(3):
            term = lax.dot_general(stack[field, row * width:row * width + pixels], grads,
                                   (((0,), (0,)), ((), ())), preferred_element_type=jnp.float32)
            rows = slice(row * triple, (row + 1) * triple)
            if tick > 0:
                term = total[index, rows] + term
            total[index, rows] = term
            if tick == ticks - 1:
                total_half[index, rows] = term.astype(jnp.bfloat16)

    def flip(index):
        for tap in range(9):
            back = 8 - tap
            flipped[index, tap * channels:(tap + 1) * channels] = (
                wts[index, back * channels:(back + 1) * channels].T)

    def act(value):
        wide = value.astype(jnp.float32)
        return (wide * jax.nn.sigmoid(wide)).astype(jnp.bfloat16)

    def slope(value):
        wide = value.astype(jnp.float32)
        sigmoid = jax.nn.sigmoid(wide)
        return sigmoid * (1.0 + wide * (1.0 - sigmoid))

    def move_copy(tick, field):
        other = seg + 1 if field < RET1 else seg - 1
        return pltpu.make_async_remote_copy(
            src_ref=sent.at[tick, field], dst_ref=landing(tick, field),
            send_sem=move_send.at[tick, field], recv_sem=move_recv.at[tick, field],
            device_id=(other, band), device_id_type=MESH)

    def send_on(tick, field, value):
        sent[tick, field] = value
        if field < RET1:
            pl.when(seg < segments - 1)(move_copy(tick, field).start)

            @pl.when(last_seg)
            def _():
                landing(tick, field + RET1)[...] = value
        else:
            pl.when(seg > 0)(move_copy(tick, field).start)

    def take(tick, fields):
        for field in fields:
            if field < RET1:
                pl.when(seg > 0)(move_copy(tick, field).wait_recv)
            else:
                pl.when(seg < segments - 1)(move_copy(tick, field).wait_recv)
        fresh_copy, loss_copy = edge_copies(tick)
        if FWD1 in fields:
            pl.when(first_seg)(fresh_copy.wait)
        if GRD1 in fields:
            pl.when(last_seg)(loss_copy.wait)

    def reduce_copy(step, index):
        other = lax.rem(band + step, bands)
        rows = pl.ds(pl.multiple_of(other * chunk, chunk), chunk)
        return pltpu.make_async_remote_copy(
            src_ref=total_half.at[index, rows], dst_ref=partial.at[step - 1, index],
            send_sem=red_send.at[step - 1, index], recv_sem=red_recv.at[step - 1, index],
            device_id=(seg, other), device_id_type=MESH)

    def send_sums(index):
        for step in range(1, bands):
            reduce_copy(step, index).start()

    def begin(tick, field, value):
        prepare(tick, field, value)
        if tick == 0 and not entered:
            waiting.append(field)
        else:
            send_halo(tick, field)
        fill(field, width, value)

    entered, waiting = [], []
    for tick in range(ticks):
        if tick == 0:
            p, q = fwd_v.at[0], fwd_v.at[1]
            y1, y2 = ret_v.at[0], ret_v.at[1]
            g1, g2 = grd_v.at[0], grd_v.at[1]
            loads[0].wait()
        else:
            p, q, y1, y2, g1, g2 = (came.at[tick - 1, field] for field in range(6))
            take(tick - 1, (FWD1, FWD2))
        begin(tick, ACT_Q, act(q[...]))
        if tick == 0:
            loads[1].wait()
            begin(tick, ACT_Y, act(y1[...]))
            loads[2].wait()
            begin(tick, GRAD2, g2[...])
            others = (seg > 0).astype(jnp.int32) + (seg < segments - 1).astype(jnp.int32)
            pl.semaphore_wait(barrier, bands - 1 + others)
            entered.append(True)
            for field in waiting:
                send_halo(tick, field)
            loads[3].wait()

        def advance_first():
            take_halo(tick, ACT_Q)
            out1 = (p[...].astype(jnp.float32) + apply(ACT_Q, wts.at[0])).astype(jnp.bfloat16)
            send_on(tick, FWD1, out1)
            begin(tick, ACT_OUT, act(out1))

        def advance_second():
            take_halo(tick, ACT_OUT)
            out2 = (q[...].astype(jnp.float32) + apply(ACT_OUT, wts.at[1])).astype(jnp.bfloat16)
            send_on(tick, FWD2, out2)

        advance_first()
        if tick == 0:
            loads[4].wait()
        else:
            advance_second()
            take(tick - 1, (RET1, RET2, GRD1, GRD2))
            begin(tick, ACT_Y, act(y1[...]))
            begin(tick, GRAD2, g2[...])
        take_halo(tick, ACT_Y)
        q2 = (y2[...].astype(jnp.float32) - apply(ACT_Y, wts.at[1])).astype(jnp.bfloat16)
        send_on(tick, RET2, q2)
        begin(tick, ACT_IN, act(q2))
        take_halo(tick, GRAD2)
        if tick == 0:
            flip(1)
        h1 = (g1[...].astype(jnp.float32) + slope(y1[...]) * apply(GRAD2, flipped.at[1])).astype(jnp.bfloat16)
        send_on(tick, GRD1, h1)
        begin(tick, BACK1, h1)
        if tick == 0:
            advance_second()
            flip(0)
        take_halo(tick, ACT_IN)
        p2 = (y1[...].astype(jnp.float32) - apply(ACT_IN, wts.at[0])).astype(jnp.bfloat16)
        send_on(tick, RET1, p2)
        take_halo(tick, BACK1)
        h2 = (g2[...].astype(jnp.float32)
              + slope(sent[tick, RET2]) * apply(BACK1, flipped.at[0])).astype(jnp.bfloat16)
        send_on(tick, GRD2, h2)
        correlate(tick, 1, ACT_Y, g2[...])
        if tick == ticks - 1:
            send_sums(1)
        correlate(tick, 0, ACT_IN, sent[tick, GRD1])
        if tick == ticks - 1:
            send_sums(0)

    own = pl.ds(pl.multiple_of(band * chunk, chunk), chunk)
    for index in (1, 0):
        for step in range(1, bands):
            reduce_copy(step, index).wait_recv()
        value = total[index, own]
        for step in range(1, bands):
            value = value + partial[step - 1, index].astype(jnp.float32)
        wgrad_out[index] = value
    take(ticks - 1, range(6))
    for index in (1, 0):
        for step in range(1, bands):
            reduce_copy(step, index).wait_send()
    for tick in range(ticks):
        for field in range(6):
            pl.when(band > 0)(halo_copy(tick, field, 0).wait_send)
            pl.when(band < bands - 1)(halo_copy(tick, field, 1).wait_send)
            if field < RET1:
                pl.when(seg < segments - 1)(move_copy(tick, field).wait_send)
            else:
                pl.when(seg > 0)(move_copy(tick, field).wait_send)


def local(forward_state, returning_state, returning_grad, weights, fresh_input, loss_grad):
    segments, bands = lax.axis_size("segment"), lax.axis_size("band")
    _, _, rows, width, channels = forward_state.shape
    pixels = rows * width
    ticks = fresh_input.shape[0]
    taps = weights.shape[2]
    chunk = taps // bands
    bf16, f32 = jnp.bfloat16, jnp.float32
    pair = jax.ShapeDtypeStruct((2, pixels, channels), bf16)
    dma = pltpu.SemaphoreType.DMA
    flat = lambda x: x.reshape(x.shape[:-3] + (pixels, channels))
    vmem = pl.BlockSpec(memory_space=pltpu.VMEM)
    outs = pl.pallas_call(
        functools.partial(kernel, ticks, segments, bands, width),
        out_shape=(pair, pair, pair, jax.ShapeDtypeStruct((2, chunk, channels), f32)),
        in_specs=[pl.BlockSpec(memory_space=pl.ANY)] * 6,
        out_specs=(vmem,) * 4,
        scratch_shapes=[
            pltpu.VMEM((2, pixels, channels), bf16),
            pltpu.VMEM((2, pixels, channels), bf16),
            pltpu.VMEM((2, pixels, channels), bf16),
            pltpu.VMEM((2, taps, channels), bf16),
            pltpu.VMEM((2, taps, channels), bf16),
            pltpu.VMEM((6, pixels + 2 * width, 3 * channels), bf16),
            pltpu.VMEM((ticks, 6, 2, width, channels), bf16),
            pltpu.VMEM((ticks, 6, 2, width, channels), bf16),
            pltpu.VMEM((ticks, 6, pixels, channels), bf16),
            pltpu.VMEM((max(ticks - 1, 1), 6, pixels, channels), bf16),
            pltpu.VMEM((2, taps, channels), f32),
            pltpu.VMEM((2, taps, channels), bf16),
            pltpu.VMEM((bands - 1, 2, chunk, channels), bf16),
            dma((5,)),
            dma((ticks, 2)),
            dma((ticks, 6, 2)),
            dma((ticks, 6, 2)),
            dma((ticks, 6)),
            dma((ticks, 6)),
            dma((bands - 1, 2)),
            dma((bands - 1, 2)),
        ],
        compiler_params=pltpu.CompilerParams(
            collective_id=0, has_side_effects=True, vmem_limit_bytes=60 * 2**20),
    )(flat(forward_state[0]), flat(returning_state[0]), flat(returning_grad[0]), weights[0],
      flat(fresh_input), flat(loss_grad))
    shape = forward_state.shape
    return tuple(o.reshape(shape) for o in outs[:3]) + (outs[3][None],)


def solution(mesh):
    pair = P("segment", None, "band", None, None)
    whole = P(None, None, "band", None, None)
    return jax.shard_map(
        local,
        mesh=mesh,
        in_specs=(pair, pair, pair, P("segment", None, None, None), whole, whole),
        out_specs=(pair, pair, pair, P("segment", None, "band", None)),
        check_vma=False,
    )
```

time: 185 us -> 93.7 us (0.51)
  the two profiles are of different devices: /device:TPU:9 before, /device:TPU:15 now
where the time goes in v1:
time: 93.7 us; the launch traced here: 93.5 us
  Pallas kernels  88.3 us (94%)
  local copies, waits for them, and re-layouts  4.58 us (5%)
    pallas_call x1, Pallas kernels, local(): pl.pallas_call(functools.partial(kernel, ticks, segments, bands, width),...  88.3 us
    unnamed x10, local copies, waits for them, and re-layouts  4.58 us

profile of v1, /device:TPU:15, one launch (start us, length us, event | category | flops | bytes accessed | tf_op | source)
XLA Modules:
  0.0 93.5 jit_solution(15985026093652242089)
XLA Ops:
  0.6 88.3 %shard_map.93 = (bf16[2,512,256]{2,1,0:T(8,128)(2,1)}, bf16[2,512,256]{2,1,0:T(8,128)(2,1)}, bf16[2,512,256]{2,1,0:T(8,128)(2,1)}, f32[2,576,256]{2,1,0:T(8,128)}) custom-call(bf16[2,512,256]{2,1,0:T(8,128)(2,1)} %bitcast.14, bf16[2,512,256]{2,1,0:T(8,128)(2,1)} %bitcast.15, bf16[2,512,256]{2,1,0:T(8,128)(2,1)} %bitcast.16, bf16[2,2304,256]{2,1,0:T(8,128)(2,1)} %bitcast.10, ...), custom_call_target="tpu_custom_call" | custom-call | tf_op jit(solution)/shard_map/pallas_call | solution.py:304
  88.9 0.0 copy-start.2
  89.0 0.0 copy-start.1
  89.0 2.0 %copy.14 = bf16[1,2,8,64,256]{4,3,2,1,0:T(8,128)(2,1)} copy(bf16[1,2,8,64,256]{4,3,2,1,0:T(8,128)(2,1)} %bitcast.19) | data formatting | bytes 1048576
  90.9 0.0 copy-done.2
  90.9 0.0 copy-start
  90.9 0.8 copy.15
  91.7 0.0 copy-done.1
  91.7 0.8 copy.16
  92.5 0.0 copy-done
  92.5 1.0 %copy.17 = f32[1,2,576,256]{3,2,1,0:T(8,128)} copy(f32[1,2,576,256]{3,2,1,0:T(8,128)S(1)} %bitcast.11) | data formatting | bytes 2359296
Async XLA Ops:
  88.9 2.0 %copy-start.2 = (bf16[2,512,256]{2,1,0:T(8,128)(2,1)S(1)}, bf16[2,512,256]{2,1,0:T(8,128)(2,1)}, u32[]{:S(2)}) copy-start(bf16[2,512,256]{2,1,0:T(8,128)(2,1)} %get-tuple-element.9) | copy-start | bytes 1572868
  89.0 2.8 %copy-start.1 = (bf16[2,512,256]{2,1,0:T(8,128)(2,1)S(1)}, bf16[2,512,256]{2,1,0:T(8,128)(2,1)}, u32[]{:S(2)}) copy-start(bf16[2,512,256]{2,1,0:T(8,128)(2,1)} %get-tuple-element.10) | copy-start | bytes 1572868
  90.9 1.6 %copy-start = (f32[2,576,256]{2,1,0:T(8,128)S(1)}, f32[2,576,256]{2,1,0:T(8,128)}, u32[]{:S(2)}) copy-start(f32[2,576,256]{2,1,0:T(8,128)} %get-tuple-element.11) | copy-start | bytes 3538948

commit v2 on v1

--- a/solution.py
+++ b/solution.py
@@ -14,8 +14,9 @@
 
 def kernel(ticks, segments, bands, width, fwd_in, ret_in, grd_in, weights_in, fresh_in, loss_in,
            fwd_out, ret_out, grd_out, wgrad_out,
-           fwd_v, ret_v, grd_v, wts, flipped, stack, halo_src, halo_dst, sent, came, total, total_half, partial,
-           in_sem, edge_sem, halo_send, halo_recv, move_send, move_recv, red_send, red_recv):
+           fwd_v, ret_v, grd_v, wts, flipped, stack, halo_src, halo_dst, sent, came, total, total_half, paired, reduced, partial,
+           in_sem, edge_sem, halo_send, halo_recv, move_send, move_recv, pair_send, pair_recv,
+           red_send, red_recv):
     seg = lax.axis_index("segment")
     band = lax.axis_index("band")
     pixels = fwd_v.shape[1]
@@ -83,10 +84,6 @@
             src_ref=halo_src.at[tick, field, side], dst_ref=halo_dst.at[tick, field, 1 - side],
             send_sem=halo_send.at[tick, field, side], recv_sem=halo_recv.at[tick, field, 1 - side],
             device_id=(seg, band - 1 if side == 0 else band + 1), device_id_type=MESH)
-
-    def prepare(tick, field, value):
-        halo_src[tick, field, 0] = value[:width]
-        halo_src[tick, field, 1] = value[pixels - width:]
 
     def send_halo(tick, field):
         pl.when(band > 0)(halo_copy(tick, field, 0).start)
@@ -178,107 +175,150 @@
         if GRD1 in fields:
             pl.when(last_seg)(loss_copy.wait)
 
-    def reduce_copy(step, index):
-        other = lax.rem(band + step, bands)
-        rows = pl.ds(pl.multiple_of(other * chunk, chunk), chunk)
+    groups = bands // 2
+    core, group = lax.rem(band, 2), band // 2
+
+    def chunk_rows(owner):
+        return pl.ds(pl.multiple_of(owner * chunk, chunk), chunk)
+
+    def pair_copy(index, target):
         return pltpu.make_async_remote_copy(
-            src_ref=total_half.at[index, rows], dst_ref=partial.at[step - 1, index],
-            send_sem=red_send.at[step - 1, index], recv_sem=red_recv.at[step - 1, index],
+            src_ref=total_half.at[index, chunk_rows(2 * target + 1 - core)], dst_ref=paired.at[index, target],
+            send_sem=pair_send.at[index, target], recv_sem=pair_recv.at[index, target],
+            device_id=(seg, band + 1 - 2 * core), device_id_type=MESH)
+
+    def reduce_copy(index, step):
+        other = 2 * lax.rem(group + step, groups) + core
+        return pltpu.make_async_remote_copy(
+            src_ref=reduced.at[index, step - 1], dst_ref=partial.at[index, step - 1],
+            send_sem=red_send.at[index, step - 1], recv_sem=red_recv.at[index, step - 1],
             device_id=(seg, other), device_id_type=MESH)
 
-    def send_sums(index):
-        for step in range(1, bands):
-            reduce_copy(step, index).start()
-
-    def begin(tick, field, value):
-        prepare(tick, field, value)
-        if tick == 0 and not entered:
-            waiting.append(field)
-        else:
-            send_halo(tick, field)
-        fill(field, width, value)
-
-    entered, waiting = [], []
+    def start_sums(index):
+        for target in range(groups):
+            pair_copy(index, target).start()
+
+    def pair_sum(index, target):
+        return total[index, chunk_rows(2 * target + core)] + paired[index, target].astype(jnp.float32)
+
+    def pass_sums(index):
+        for target in range(groups):
+            pair_copy(index, target).wait_recv()
+        for step in range(1, groups):
+            reduced[index, step - 1] = pair_sum(index, lax.rem(group + step, groups)).astype(jnp.bfloat16)
+            reduce_copy(index, step).start()
+
+    def finish_sums(index):
+        value = pair_sum(index, group)
+        for step in range(1, groups):
+            reduce_copy(index, step).wait_recv()
+            value = value + partial[index, step - 1].astype(jnp.float32)
+        wgrad_out[index] = value
+
+    def begin(tick, field, ref, function):
+        halo_src[tick, field, 0] = function(ref[0:width])
+        halo_src[tick, field, 1] = function(ref[pixels - width:pixels])
+        send_halo(tick, field)
+        fill(field, width, function(ref[...]))
+
     for tick in range(ticks):
+        last_tick = tick == ticks - 1
         if tick == 0:
             p, q = fwd_v.at[0], fwd_v.at[1]
             y1, y2 = ret_v.at[0], ret_v.at[1]
             g1, g2 = grd_v.at[0], grd_v.at[1]
-            loads[0].wait()
         else:
             p, q, y1, y2, g1, g2 = (came.at[tick - 1, field] for field in range(6))
-            take(tick - 1, (FWD1, FWD2))
-        begin(tick, ACT_Q, act(q[...]))
-        if tick == 0:
-            loads[1].wait()
-            begin(tick, ACT_Y, act(y1[...]))
-            loads[2].wait()
-            begin(tick, GRAD2, g2[...])
-            others = (seg > 0).astype(jnp.int32) + (seg < segments - 1).astype(jnp.int32)
-            pl.semaphore_wait(barrier, bands - 1 + others)
-            entered.append(True)
-            for field in waiting:
-                send_halo(tick, field)
-            loads[3].wait()
+
+        def same(value):
+            return value
 
         def advance_first():
             take_halo(tick, ACT_Q)
             out1 = (p[...].astype(jnp.float32) + apply(ACT_Q, wts.at[0])).astype(jnp.bfloat16)
             send_on(tick, FWD1, out1)
-            begin(tick, ACT_OUT, act(out1))
+            begin(tick, ACT_OUT, sent.at[tick, FWD1], act)
 
         def advance_second():
             take_halo(tick, ACT_OUT)
             out2 = (q[...].astype(jnp.float32) + apply(ACT_OUT, wts.at[1])).astype(jnp.bfloat16)
             send_on(tick, FWD2, out2)
 
-        advance_first()
+        def invert_second():
+            take_halo(tick, ACT_Y)
+            q2 = (y2[...].astype(jnp.float32) - apply(ACT_Y, wts.at[1])).astype(jnp.bfloat16)
+            send_on(tick, RET2, q2)
+            begin(tick, ACT_IN, sent.at[tick, RET2], act)
+
+        def invert_first():
+            take_halo(tick, ACT_IN)
+            p2 = (y1[...].astype(jnp.float32) - apply(ACT_IN, wts.at[0])).astype(jnp.bfloat16)
+            send_on(tick, RET1, p2)
+
+        def back_first():
+            take_halo(tick, GRAD2)
+            h1 = (g1[...].astype(jnp.float32) + slope(y1[...]) * apply(GRAD2, flipped.at[1])).astype(jnp.bfloat16)
+            send_on(tick, GRD1, h1)
+            begin(tick, BACK1, sent.at[tick, GRD1], same)
+
+        def back_second():
+            take_halo(tick, BACK1)
+            h2 = (g2[...].astype(jnp.float32)
+                  + slope(sent[tick, RET2]) * apply(BACK1, flipped.at[0])).astype(jnp.bfloat16)
+            send_on(tick, GRD2, h2)
+
         if tick == 0:
+            loads[0].wait()
+            others = (seg > 0).astype(jnp.int32) + (seg < segments - 1).astype(jnp.int32)
+            pl.semaphore_wait(barrier, bands - 1 + others)
+            begin(tick, ACT_Q, q, act)
+            loads[1].wait()
+            begin(tick, ACT_Y, y1, act)
+            loads[3].wait()
+            advance_first()
+            loads[2].wait()
+            begin(tick, GRAD2, g2, same)
             loads[4].wait()
+            invert_second()
+            advance_second()
+            flip(1)
+            back_first()
+            invert_first()
+            flip(0)
+            back_second()
         else:
+            take(tick - 1, (FWD1, FWD2))
+            begin(tick, ACT_Q, q, act)
+            advance_first()
             advance_second()
-            take(tick - 1, (RET1, RET2, GRD1, GRD2))
-            begin(tick, ACT_Y, act(y1[...]))
-            begin(tick, GRAD2, g2[...])
-        take_halo(tick, ACT_Y)
-        q2 = (y2[...].astype(jnp.float32) - apply(ACT_Y, wts.at[1])).astype(jnp.bfloat16)
-        send_on(tick, RET2, q2)
-        begin(tick, ACT_IN, act(q2))
-        take_halo(tick, GRAD2)
-        if tick == 0:
-            flip(1)
-        h1 = (g1[...].astype(jnp.float32) + slope(y1[...]) * apply(GRAD2, flipped.at[1])).astype(jnp.bfloat16)
-        send_on(tick, GRD1, h1)
-        begin(tick, BACK1, h1)
-        if tick == 0:
-            advance_second()
-            flip(0)
-        take_halo(tick, ACT_IN)
-        p2 = (y1[...].astype(jnp.float32) - apply(ACT_IN, wts.at[0])).astype(jnp.bfloat16)
-        send_on(tick, RET1, p2)
-        take_halo(tick, BACK1)
-        h2 = (g2[...].astype(jnp.float32)
-              + slope(sent[tick, RET2]) * apply(BACK1, flipped.at[0])).astype(jnp.bfloat16)
-        send_on(tick, GRD2, h2)
+            take(tick - 1, (RET1, RET2))
+            begin(tick, ACT_Y, y1, act)
+            invert_second()
+            take(tick - 1, (GRD1, GRD2))
+            begin(tick, GRAD2, g2, same)
+            back_first()
         correlate(tick, 1, ACT_Y, g2[...])
-        if tick == ticks - 1:
-            send_sums(1)
+        if last_tick:
+            start_sums(1)
+        if tick > 0:
+            invert_first()
         correlate(tick, 0, ACT_IN, sent[tick, GRD1])
-        if tick == ticks - 1:
-            send_sums(0)
-
-    own = pl.ds(pl.multiple_of(band * chunk, chunk), chunk)
-    for index in (1, 0):
-        for step in range(1, bands):
-            reduce_copy(step, index).wait_recv()
-        value = total[index, own]
-        for step in range(1, bands):
-            value = value + partial[step - 1, index].astype(jnp.float32)
-        wgrad_out[index] = value
+        if last_tick:
+            start_sums(0)
+        if tick > 0:
+            back_second()
+        if last_tick:
+            pass_sums(1)
+            pass_sums(0)
+
+    finish_sums(1)
+    finish_sums(0)
     take(ticks - 1, range(6))
-    for index in (1, 0):
-        for step in range(1, bands):
-            reduce_copy(step, index).wait_send()
+    for index in range(2):
+        for target in range(groups):
+            pair_copy(index, target).wait_send()
+        for step in range(1, groups):
+            reduce_copy(index, step).wait_send()
     for tick in range(ticks):
         for field in range(6):
             pl.when(band > 0)(halo_copy(tick, field, 0).wait_send)
@@ -287,6 +327,16 @@
                 pl.when(seg < segments - 1)(move_copy(tick, field).wait_send)
             else:
                 pl.when(seg > 0)(move_copy(tick, field).wait_send)
+
+
+def store(*refs):
+    count = len(refs) // 2
+    sems = refs[-1]
+    copies = [pltpu.make_async_copy(refs[i], refs[count + i], sems.at[i]) for i in range(count)]
+    for copy in copies:
+        copy.start()
+    for copy in copies:
+        copy.wait()
 
 
 def local(forward_state, returning_state, returning_grad, weights, fresh_input, loss_grad):
@@ -319,20 +369,31 @@
             pltpu.VMEM((max(ticks - 1, 1), 6, pixels, channels), bf16),
             pltpu.VMEM((2, taps, channels), f32),
             pltpu.VMEM((2, taps, channels), bf16),
-            pltpu.VMEM((bands - 1, 2, chunk, channels), bf16),
+            pltpu.VMEM((2, bands // 2, chunk, channels), bf16),
+            pltpu.VMEM((2, bands // 2 - 1, chunk, channels), bf16),
+            pltpu.VMEM((2, bands // 2 - 1, chunk, channels), bf16),
             dma((5,)),
             dma((ticks, 2)),
             dma((ticks, 6, 2)),
             dma((ticks, 6, 2)),
             dma((ticks, 6)),
             dma((ticks, 6)),
-            dma((bands - 1, 2)),
-            dma((bands - 1, 2)),
+            dma((2, bands // 2)),
+            dma((2, bands // 2)),
+            dma((2, bands // 2 - 1)),
+            dma((2, bands // 2 - 1)),
         ],
         compiler_params=pltpu.CompilerParams(
             collective_id=0, has_side_effects=True, vmem_limit_bytes=60 * 2**20),
     )(flat(forward_state[0]), flat(returning_state[0]), flat(returning_grad[0]), weights[0],
       flat(fresh_input), flat(loss_grad))
+    outs = pl.pallas_call(
+        store,
+        out_shape=tuple(jax.ShapeDtypeStruct(o.shape, o.dtype) for o in outs),
+        in_specs=[vmem] * 4,
+        out_specs=(pl.BlockSpec(memory_space=pl.ANY),) * 4,
+        scratch_shapes=[dma((4,))],
+    )(*outs)
     shape = forward_state.shape
     return tuple(o.reshape(shape) for o in outs[:3]) + (outs[3][None],)
 

time: 93.7 us -> 109 us (1.16)
  the two profiles are of different devices: /device:TPU:15 before, /device:TPU:9 now
where the time goes in v2:
time: 109 us
  Pallas kernels  109 us (100%)
    pallas_call x1, Pallas kernels, local(): pl.pallas_call(functools.partial(kernel, ticks, segments, bands, width),...  105 us
    pallas_call x1, Pallas kernels, local(): pl.pallas_call(store, out_shape=tuple((jax.ShapeDtypeStruct(o.shape, o.dt...  3.32 us

profile of v2, /device:TPU:9, one launch (start us, length us, event | category | flops | bytes accessed | tf_op | source)
XLA Modules:
  0.0 109.3 jit_solution(14568841411494804440)
XLA Ops:
  0.6 105.2 %shard_map.93 = (bf16[2,512,256]{2,1,0:T(8,128)(2,1)}, bf16[2,512,256]{2,1,0:T(8,128)(2,1)}, bf16[2,512,256]{2,1,0:T(8,128)(2,1)}, f32[2,576,256]{2,1,0:T(8,128)}) custom-call(bf16[2,512,256]{2,1,0:T(8,128)(2,1)} %bitcast.13, bf16[2,512,256]{2,1,0:T(8,128)(2,1)} %bitcast.14, bf16[2,512,256]{2,1,0:T(8,128)(2,1)} %bitcast.15, bf16[2,2304,256]{2,1,0:T(8,128)(2,1)} %bitcast.10, ...), custom_call_target="tpu_custom_call" | custom-call | tf_op jit(solution)/shard_map/pallas_call | solution.py:354
  105.8 3.3 %shard_map.94 = (bf16[2,512,256]{2,1,0:T(8,128)(2,1)}, bf16[2,512,256]{2,1,0:T(8,128)(2,1)}, bf16[2,512,256]{2,1,0:T(8,128)(2,1)}, f32[2,576,256]{2,1,0:T(8,128)}) custom-call(bf16[2,512,256]{2,1,0:T(8,128)(2,1)} %get-tuple-element.12.refs_0_, bf16[2,512,256]{2,1,0:T(8,128)(2,1)} %get-tuple-element.13.refs_1_, ...), custom_call_target="tpu_custom_call" | custom-call | tf_op jit(solution)/shard_map/pallas_call | solution.py:390

commit v3 on v2

--- a/solution.py
+++ b/solution.py
@@ -291,11 +291,10 @@
             begin(tick, ACT_Q, q, act)
             advance_first()
             advance_second()
-            take(tick - 1, (RET1, RET2))
+            take(tick - 1, (RET1, RET2, GRD1, GRD2))
             begin(tick, ACT_Y, y1, act)
+            begin(tick, GRAD2, g2, same)
             invert_second()
-            take(tick - 1, (GRD1, GRD2))
-            begin(tick, GRAD2, g2, same)
             back_first()
         correlate(tick, 1, ACT_Y, g2[...])
         if last_tick:
@@ -330,13 +329,18 @@
 
 
 def store(*refs):
-    count = len(refs) // 2
-    sems = refs[-1]
-    copies = [pltpu.make_async_copy(refs[i], refs[count + i], sems.at[i]) for i in range(count)]
-    for copy in copies:
-        copy.start()
-    for copy in copies:
-        copy.wait()
+    count = (len(refs) - 2) // 3
+    sources, targets, held = refs[:count], refs[count:2 * count], refs[2 * count:3 * count]
+    load_sem, store_sem = refs[3 * count:]
+    loads = [pltpu.make_async_copy(sources[i], held[i], load_sem.at[i]) for i in range(count)]
+    stores = [pltpu.make_async_copy(held[i], targets[i], store_sem.at[i]) for i in range(count)]
+    for load in loads:
+        load.start()
+    for load, out in zip(loads, stores):
+        load.wait()
+        out.start()
+    for out in stores:
+        out.wait()
 
 
 def local(forward_state, returning_state, returning_grad, weights, fresh_input, loss_grad):
@@ -390,9 +394,9 @@
     outs = pl.pallas_call(
         store,
         out_shape=tuple(jax.ShapeDtypeStruct(o.shape, o.dtype) for o in outs),
-        in_specs=[vmem] * 4,
+        in_specs=[pl.BlockSpec(memory_space=pl.ANY)] * 4,
         out_specs=(pl.BlockSpec(memory_space=pl.ANY),) * 4,
-        scratch_shapes=[dma((4,))],
+        scratch_shapes=[pltpu.VMEM(o.shape, o.dtype) for o in outs] + [dma((4,)), dma((4,))],
     )(*outs)
     shape = forward_state.shape
     return tuple(o.reshape(shape) for o in outs[:3]) + (outs[3][None],)

time: 109 us -> 86.5 us (0.79)
  Pallas kernels: 109 us -> 85.6 us
    pallas_call x1, Pallas kernels: 105 us -> 82.7 us  [local(): pl.pallas_call(functools.partial(kernel, ticks, segments, bands, width),...]
where the time goes in v3:
time: 86.5 us; the launch traced here: 86.4 us
  Pallas kernels  85.6 us (99%)
    pallas_call x1, Pallas kernels, local(): pl.pallas_call(functools.partial(kernel, ticks, segments, bands, width),...  82.7 us
    pallas_call x1, Pallas kernels, local(): pl.pallas_call(store, out_shape=tuple((jax.ShapeDtypeStruct(o.shape, o.dt...  2.84 us

profile of v3, /device:TPU:9, one launch (start us, length us, event | category | flops | bytes accessed | tf_op | source)
XLA Modules:
  0.0 86.4 jit_solution(5520058149305290481)
XLA Ops:
  0.6 82.7 %shard_map.93 = (bf16[2,512,256]{2,1,0:T(8,128)(2,1)}, bf16[2,512,256]{2,1,0:T(8,128)(2,1)}, bf16[2,512,256]{2,1,0:T(8,128)(2,1)}, f32[2,576,256]{2,1,0:T(8,128)}) custom-call(bf16[2,512,256]{2,1,0:T(8,128)(2,1)} %bitcast.13, bf16[2,512,256]{2,1,0:T(8,128)(2,1)} %bitcast.14, bf16[2,512,256]{2,1,0:T(8,128)(2,1)} %bitcast.15, bf16[2,2304,256]{2,1,0:T(8,128)(2,1)} %bitcast.10, ...), custom_call_target="tpu_custom_call" | custom-call | tf_op jit(solution)/shard_map/pallas_call | solution.py:358
  83.4 2.8 %shard_map.94 = (bf16[2,512,256]{2,1,0:T(8,128)(2,1)}, bf16[2,512,256]{2,1,0:T(8,128)(2,1)}, bf16[2,512,256]{2,1,0:T(8,128)(2,1)}, f32[2,576,256]{2,1,0:T(8,128)}) custom-call(bf16[2,512,256]{2,1,0:T(8,128)(2,1)} %get-tuple-element.12.refs_0_, bf16[2,512,256]{2,1,0:T(8,128)(2,1)} %get-tuple-element.13.refs_1_, ...), custom_call_target="tpu_custom_call" | custom-call | tf_op jit(solution)/shard_map/pallas_call | solution.py:394
